TPU v7x, 768 devices: a whole 4x8x12 slice. The times are simulated.
768 devices in a mesh: slab: 12 (over z_lo, core), row: 64 (over x, y, z_hi).
Axes of the slice: x: 4, y: 8, z: 12 (z_hi: 2, z_lo: 6; z = z_hi * 6 + z_lo), core: 2. Of those that a mesh axis runs over, the one named last changes fastest.
Arguments:
- velocity: bfloat16 [512, 96, 3, 1536], P('row', 'slab'), may hold values from -6 to 6
- deriv_x: bfloat16 [1536, 1536], replicated, may hold values from -0.15625 to 0.15625
- deriv_y: bfloat16 [512, 512], replicated, may hold values from -0.25 to 0.25
- metric_x: float32 [1536], replicated, may hold values from 0.5 to 2
- metric_y: float32 [512], replicated, may hold values from 0.5 to 2
- coarse_force: bfloat16 [128, 48, 3, 192], P('row', 'slab'), may hold values from -6 to 6
- row_map: int32 [512], P('row'), may hold values from 0 to 127, as said below
- x_index: int32 [1536], replicated, may hold values from 0 to 190, as said below
- x_weight: bfloat16 [1536], replicated, may hold values from 0 to 1
Outputs:
- tendency: bfloat16 [512, 96, 3, 1536], P('row', 'slab')
- updated: bfloat16 [512, 96, 3, 1536], P('row', 'slab')
Inputs may be any that keep to these rules, and one draw needn't show every extreme that they name: `row_map`: each coarse row is named by exactly 4 fine rows. `x_index`: every value of the range is named by some fine column.
All inputs are finite; a program needn't handle non-finite values.
Results may differ from a plain program's by a relative error of at most 0.004.
Values may be sent and summed in bfloat16 or wider, within the bound.
A program may use at most 32 MiB of HBM per device.

v0:
```python
import jax
import jax.numpy as jnp
from jax import lax
from jax.sharding import PartitionSpec as P

rk_weight = 0.5


def passed_along(block, axis, distance):
    devices = range(lax.axis_size(axis))
    route = [(i - distance, i) for i in devices if i - distance in devices]
    return lax.ppermute(block, axis, route)


def refine_levels(extended):
    lower = extended[:, :-1]
    middle = (0.5 * (lower.astype(jnp.float32) + extended[:, 1:].astype(jnp.float32))).astype(
        jnp.bfloat16
    )
    stacked = jnp.stack([lower, middle], axis=2)
    return stacked.reshape(
        extended.shape[0], 2 * (extended.shape[1] - 1), extended.shape[2], extended.shape[3]
    )


def upsample_table(x_index, x_weight, coarse_width):
    positions = jnp.arange(coarse_width, dtype=jnp.int32)[:, None]
    nothing = jnp.zeros((), jnp.bfloat16)
    left_part = jnp.where(positions == x_index[None, :], x_weight[None, :], nothing)
    right_weight = (1.0 - x_weight.astype(jnp.float32)).astype(jnp.bfloat16)
    right_part = jnp.where(positions == x_index[None, :] + 1, right_weight[None, :], nothing)
    return left_part + right_part


def shards(
    velocity, deriv_x, deriv_y, metric_x, metric_y, coarse_force, row_map, x_index, x_weight
):
    rows_here, levels_here, components, fine_width = velocity.shape
    flattened = velocity.reshape(rows_here, levels_here * components * fine_width)
    columns = lax.all_to_all(flattened, "row", split_axis=1, concat_axis=0, tiled=True)
    slope_columns = (
        jnp.dot(deriv_y, columns, preferred_element_type=jnp.float32) * metric_y[:, None]
    ).astype(jnp.bfloat16)
    along_y = lax.all_to_all(slope_columns, "row", split_axis=0, concat_axis=1, tiled=True).reshape(
        velocity.shape
    )
    along_x = (
        jnp.dot(
            velocity.reshape(-1, fine_width), deriv_x, preferred_element_type=jnp.float32
        ).reshape(velocity.shape)
        * metric_x
    )
    upper_rim = passed_along(coarse_force[:, :1], "slab", -1)
    is_topmost = lax.axis_index("slab") == lax.axis_size("slab") - 1
    rim_level = jnp.where(is_topmost, coarse_force[:, -1:], upper_rim)
    extended = jnp.concatenate([coarse_force, rim_level], axis=1)
    coarse_rows = coarse_force.shape[0] * lax.axis_size("row")
    selector = (row_map[:, None] == jnp.arange(coarse_rows, dtype=jnp.int32)[None, :]).astype(
        jnp.bfloat16
    )
    fine_source = refine_levels(extended)
    portion = lax.all_gather(fine_source, "row", axis=0, tiled=True)
    gathered = jnp.dot(
        selector, portion.reshape(portion.shape[0], -1), preferred_element_type=jnp.float32
    )
    selected = gathered.astype(jnp.bfloat16).reshape((rows_here,) + fine_source.shape[1:])
    coarse_width = coarse_force.shape[3]
    table = upsample_table(x_index, x_weight, coarse_width)
    forcing = jnp.dot(
        selected.reshape(-1, coarse_width), table, preferred_element_type=jnp.float32
    ).reshape(velocity.shape)
    moving = velocity.astype(jnp.float32)
    result = forcing - (
        moving[:, :, 0:1] * along_x + moving[:, :, 1:2] * along_y.astype(jnp.float32)
    )
    return (result.astype(jnp.bfloat16), (moving + rk_weight * result).astype(jnp.bfloat16))


def solution(mesh):
    return jax.shard_map(
        shards,
        mesh=mesh,
        in_specs=(
            P("row", "slab", None, None),
            P(),
            P(),
            P(),
            P(),
            P("row", "slab", None, None),
            P("row"),
            P(),
            P(),
        ),
        out_specs=(P("row", "slab", None, None), P("row", "slab", None, None)),
        check_vma=False,
    )
```

profile of v0, /device:TPU:1, one launch (start us, length us, event | category | flops | bytes accessed | tf_op | source)
XLA Modules:
  0.0 233.4 jit_solution(1059315281825527105)
XLA Ops:
  7.2 0.0 copy-start
  7.2 1.5 copy.24
  8.7 0.9 all_to_all.24
  9.6 0.0 copy-start.3
  9.6 0.0 copy-start.8
  9.6 1.2 copy.25
  10.8 23.8 %all-to-all-start = ((bf16[8,64,576]{2,0,1:T(8,128)(2,1)}), bf16[8,64,576]{2,0,1:T(8,128)(2,1)S(1)}, u32[]{:S(2)}, u32[]{:S(2)}) async-start(bf16[8,64,576]{2,0,1:T(8,128)(2,1)} %copy.25), calls=%async_computation | async-start | bytes 1310720 | tf_op jit(solution)/shard_map/all_to_all | solution.py:40
  34.6 0.0 all-gather.2.cloned.1.call-start
  34.7 0.0 copy-done.3
  34.7 2.9 %collective-permute-start = (bf16[2,1,3,192]{3,1,2,0:T(2,128)(2,1)S(1)}, bf16[2,1,3,192]{3,1,2,0:T(2,128)(2,1)S(1)}, u32[]{:S(2)}, u32[]{:S(2)}) collective-permute-start(bf16[2,1,3,192]{3,1,2,0:T(2,128)(2,1)S(1)} %slice.16), channel_id=1, source_target_pairs={{64,0},{128,64},{192,128},{256,192},{320,256},{384,320},{448,384},... | collective-permute-start | bytes 6920 | tf_op jit(solution)/shard_map/ppermute | solution.py:12
  37.6 20.0 %collective-permute-done = bf16[2,1,3,192]{3,1,2,0:T(2,128)(2,1)S(1)} collective-permute-done((bf16[2,1,3,192]{3,1,2,0:T(2,128)(2,1)S(1)}, bf16[2,1,3,192]{3,1,2,0:T(2,128)(2,1)S(1)}, u32[]{:S(2)}, u32[]{:S(2)}) %collective-permute-start) | collective-permute-done | bytes 2336 | tf_op jit(solution)/shard_map/ppermute | solution.py:12
  57.7 0.6 copy.21
  58.4 0.0 all-gather.2.cloned.1.call-update
  58.4 0.0 all-to-all-done
  58.4 0.0 copy-done
  58.4 0.0 copy-done.8
  58.4 0.5 fusion.11
  58.9 0.0 copy-start.1
  59.0 1.1 copy.26
  60.0 17.8 %all-to-all-start.1 = ((bf16[64,8,576]{2,1,0:T(8,128)(2,1)}), bf16[64,8,576]{2,1,0:T(8,128)(2,1)S(1)}, u32[]{:S(2)}, u32[]{:S(2)}) async-start(bf16[64,8,576]{2,1,0:T(8,128)(2,1)} %bitcast.12), calls=%async_computation.1 | async-start | bytes 1310720 | tf_op jit(solution)/shard_map/all_to_all | solution.py:44
  77.8 0.0 copy-done.1
  77.8 0.0 copy-start.6
  77.8 0.0 copy-start.4
  77.8 0.1 convert_element_type.46
  78.0 0.5 copy-done.6
  78.5 0.0 copy-done.4
  78.5 0.8 slice_bitcast_fusion.1
  79.3 0.0 copy-start.7
  79.3 136.2 %all-gather.2.cloned.1.call-done = bf16[128,8,3,192]{3,1,2,0:T(8,128)(2,1)} async-done(((bf16[2,8,3,192]{3,1,2,0:T(8,128)(2,1)}), bf16[128,8,3,192]{3,1,2,0:T(8,128)(2,1)}) %all-gather.2.cloned.1.call-update) | async-done | bytes 1179664 | tf_op jit(solution)/shard_map/all_gather | solution.py:62
  215.6 2.2 copy.22
  217.8 0.0 copy-done.7
  217.8 0.4 convolution_convert_fusion
  218.3 0.2 dot_general.15
  218.4 0.0 all-to-all-done.1
  218.5 0.1 convert_bitcast_fusion
  218.5 0.3 copy.27
  218.8 0.0 copy-start.2
  218.8 0.0 copy-start.5
  218.8 2.1 reshape.39
  221.0 0.0 copy-done.2
  221.0 0.0 copy-done.5
  221.0 4.1 %fusion.8 = f32[8,8,3,1536]{3,1,2,0:T(8,128)S(1)} fusion(bf16[8,8,3,1536]{3,1,2,0:T(8,128)(2,1)S(1)} %copy-done.1, bf16[1536,1536]{1,0:T(8,128)(2,1)} %param.10, f32[8,8,3,1536]{3,2,1,0:T(4,128)} %reshape.39, f32[8,8,1536]{2,1,0:T(8,128)S(1)} %copy-done.2, f32[1536]{0:T(1024)S(1)} %copy-done.5, f32[8,8,1536]{2,1,0:T(8,128)S(1)} %get-tuple-element.4), kind=kOutput, calls=%fused_computation.6 | convolution fusion | flops 907149312 | bytes 8460288 | tf_op jit(solution)/shard_map/dot_general | solution.py:48
  225.0 1.5 add_convert_fusion
  (7 shorter events, 0.1 us)
Async XLA Ops:
  7.2 51.2 %copy-start = (bf16[512,512]{1,0:T(8,128)(2,1)S(1)}, bf16[512,512]{1,0:T(8,128)(2,1)}, u32[]{:S(2)}) copy-start(bf16[512,512]{1,0:T(8,128)(2,1)} %param.11) | copy-start | bytes 1572868
  9.6 25.1 %copy-start.3 = (bf16[2,4,3,192]{3,1,2,0:T(4,128)(2,1)S(1)}, bf16[2,4,3,192]{3,1,2,0:T(4,128)(2,1)}, u32[]{:S(2)}) copy-start(bf16[2,4,3,192]{3,1,2,0:T(4,128)(2,1)} %param.14) | copy-start | bytes 27652
  9.6 48.8 %copy-start.8 = (f32[512]{0:T(512)S(1)}, f32[512]{0:T(512)}, u32[]{:S(2)}) copy-start(f32[512]{0:T(512)} %param.13) | copy-start | bytes 6148
  10.8 47.5 %all-to-all-start = ((bf16[8,64,576]{2,0,1:T(8,128)(2,1)}), bf16[8,64,576]{2,0,1:T(8,128)(2,1)S(1)}, u32[]{:S(2)}, u32[]{:S(2)}) async-start(bf16[8,64,576]{2,0,1:T(8,128)(2,1)} %copy.25), calls=%async_computation | async-start | bytes 1310720 | tf_op jit(solution)/shard_map/all_to_all | solution.py:40
  34.6 180.9 %all-gather.2.cloned.1.call-start = ((), (), s32[]{:S(2)}) async-start(), calls=%async_computation.2 | async-start | bytes 1597440 | tf_op jit(solution)/shard_map/all_gather | solution.py:62
  34.7 22.9 %collective-permute-start = (bf16[2,1,3,192]{3,1,2,0:T(2,128)(2,1)S(1)}, bf16[2,1,3,192]{3,1,2,0:T(2,128)(2,1)S(1)}, u32[]{:S(2)}, u32[]{:S(2)}) collective-permute-start(bf16[2,1,3,192]{3,1,2,0:T(2,128)(2,1)S(1)} %slice.16), channel_id=1, source_target_pairs={{64,0},{128,64},{192,128},{256,192},{320,256},{384,320},{448,384},... | collective-permute-start | bytes 6920 | tf_op jit(solution)/shard_map/ppermute | solution.py:12
  58.9 18.9 %copy-start.1 = (bf16[8,8,3,1536]{3,1,2,0:T(8,128)(2,1)S(1)}, bf16[8,8,3,1536]{3,1,2,0:T(8,128)(2,1)}, u32[]{:S(2)}) copy-start(bf16[8,8,3,1536]{3,1,2,0:T(8,128)(2,1)} %param.9) | copy-start | bytes 1769476
  60.0 158.4 %all-to-all-start.1 = ((bf16[64,8,576]{2,1,0:T(8,128)(2,1)}), bf16[64,8,576]{2,1,0:T(8,128)(2,1)S(1)}, u32[]{:S(2)}, u32[]{:S(2)}) async-start(bf16[64,8,576]{2,1,0:T(8,128)(2,1)} %bitcast.12), calls=%async_computation.1 | async-start | bytes 1310720 | tf_op jit(solution)/shard_map/all_to_all | solution.py:44
  77.8 0.7 copy-start.6
  77.8 0.7 copy-start.4
  79.3 138.5 %copy-start.7 = (s32[8]{0:T(128)S(1)}, s32[8]{0:T(128)}, u32[]{:S(2)}) copy-start(s32[8]{0:T(128)} %param.15) | copy-start | bytes 100
  218.8 2.2 copy-start.2
  218.8 2.1 copy-start.5
Sparse Core Ops, SparseCore 0:
  58.5 157.0 all-gather.1
where the time goes:
time: 237 us; the launch traced here: 233 us
  waiting for transfers between devices  156 us (66%)
  starting transfers between devices  44.5 us (19%)
  between operations  14.3 us (6%)
  local copies, waits for them, and re-layouts  11.5 us (5%)
  matrix products  6.53 us (3%)
    all_gather x1, waiting for transfers between devices, shards(): portion = lax.all_gather(fine_source, 'row', axis=0, tiled=True)  136 us
    all_to_all x1, starting transfers between devices, shards(): lax.all_to_all(flattened, 'row', split_axis=1, concat_axis=0, tiled=True)  23.8 us
    ppermute x1, waiting for transfers between devices, passed_along(): return lax.ppermute(block, axis, route)  20 us
    all_to_all x1, starting transfers between devices, shards(): lax.all_to_all(slope_columns, 'row', split_axis=0, concat_axis=1, tiled=T...  17.8 us
  transfers between devices with their start and end apart: 4, of which 2 were waited for; matrix products, arithmetic and copies ran while one was open for 3% of the time, Pallas kernels for 0%

commit v1 on v0

v1 whole, which is shorter than its diff:
```python
import jax
import jax.numpy as jnp
from jax import lax
from jax.experimental import pallas as pl
from jax.experimental.pallas import tpu as pltpu
from jax.sharding import PartitionSpec as P

rk_weight = 0.5
MESH = pl.DeviceIdType.MESH
F32 = jnp.float32
BF16 = jnp.bfloat16

NXD, NYD = 4, 8
LANES = 128
WIDE = NXD * LANES
PIECES = 9
FORCE = PIECES


def kernel(
    v_ref, coarse_ref, rowmap_ref, dy_ref, my_ref, mx_ref, xi_ref, xw_ref, dx_hbm,
    tend_ref, upd_ref,
    dx, ybuf, xbuf, fx, fz, zbuf, rxbuf, rybuf, rim, rm_y, rm_x, ax, chosen, table, forcing,
    send, recv, dx_sem,
):
    slab = lax.axis_index("slab")
    row = lax.axis_index("row")
    slabs = lax.axis_size("slab")
    zhi = row % 2
    y = (row // 2) % NYD
    x = row // (2 * NYD)

    def at(xx, yy, zz):
        return (slab, (xx * NYD + yy) * 2 + zz)

    y_peers = [(lax.rem(y + i, NYD), at(x, lax.rem(y + i, NYD), zhi)) for i in range(1, NYD)]
    x_peers = [(lax.rem(x + i, NXD), at(lax.rem(x + i, NXD), y, zhi)) for i in range(1, NXD)]
    z_peer = at(x, y, 1 - zhi)
    below = (lax.rem(slab + slabs - 1, slabs), row)
    above = (lax.rem(slab + 1, slabs), row)

    dx_copy = pltpu.make_async_copy(dx_hbm, dx, dx_sem)
    dx_copy.start()

    barrier = pltpu.get_barrier_semaphore()
    greeted = [d for _, d in y_peers] + [d for _, d in x_peers] + [z_peer, below, above]
    for device in greeted:
        pl.semaphore_signal(barrier, inc=1, device_id=device, device_id_type=MESH)
    pl.semaphore_wait(barrier, len(greeted))

    def remote(src, dst, stage, k, device):
        pltpu.make_async_remote_copy(
            src_ref=src, dst_ref=dst, send_sem=send.at[stage, k], recv_sem=recv.at[stage, k],
            device_id=device, device_id_type=MESH,
        ).start()

    def local(src, dst, stage, k):
        pltpu.make_async_copy(src, dst, recv.at[stage, k]).start()

    def wait_for(sem, part):
        pltpu.make_async_copy(part, part, sem).wait()

    def quarter(i):
        return pl.ds(pl.multiple_of(i * LANES, LANES), LANES)

    def eighth(i):
        return pl.ds(pl.multiple_of(i * NYD, NYD), NYD)

    def start_y(k, src):
        for j, device in y_peers:
            remote(src.at[j], ybuf.at[k, y], 0, k, device)
        local(src.at[y], ybuf.at[k, y], 0, k)

    def start_x(k, dst):
        wait_for(recv.at[0, k], ybuf.at[k])
        for i, device in x_peers:
            remote(ybuf.at[k, :, :, quarter(i)], dst.at[eighth(x)], 1, k, device)
        local(ybuf.at[k, :, :, quarter(x)], dst.at[eighth(x)], 1, k)

    def start_z(k):
        wait_for(recv.at[1, k], xbuf.at[k, :, zhi])
        remote(xbuf.at[k, :, zhi], xbuf.at[k, :, zhi], 2, k, z_peer)

    def start_back_x(k):
        for i, device in x_peers:
            remote(zbuf.at[k, eighth(i)], rxbuf.at[k, :, :, quarter(x)], 3, k, device)
        local(zbuf.at[k, eighth(x)], rxbuf.at[k, :, :, quarter(x)], 3, k)

    def start_back_y(k):
        wait_for(recv.at[3, k], rxbuf.at[k])
        for j, device in y_peers:
            remote(rxbuf.at[k, j], rybuf.at[k, y], 4, k, device)
        local(rxbuf.at[k, y], rybuf.at[k, y], 4, k)

    def wait_back_y(k):
        wait_for(recv.at[4, k], rybuf.at[k])

    start_y(0, v_ref.at[0])
    start_y(FORCE, coarse_ref)
    for _, device in y_peers:
        remote(rowmap_ref, rm_y.at[y], 5, 0, device)
    local(rowmap_ref, rm_y.at[y], 5, 0)
    start_y(1, v_ref.at[1])
    start_y(2, v_ref.at[2])

    spot = lax.broadcasted_iota(jnp.int32, (NXD * NYD * 8, 512), 0)
    here = lax.broadcasted_iota(jnp.int32, (NXD * NYD * 8, 512), 1)
    mine = (spot // 8) * 16 + zhi * 8 + spot % 8
    metric = jnp.sum(jnp.where(here == mine, my_ref[...], 0.0), axis=1, keepdims=True)

    start_x(0, xbuf.at[0, :, zhi])
    start_x(FORCE, fx)
    wait_for(recv.at[5, 0], rm_y)
    for _, device in x_peers:
        remote(rm_y, rm_x.at[eighth(x)], 5, 1, device)
    local(rm_y, rm_x.at[eighth(x)], 5, 1)
    start_z(0)

    wait_for(recv.at[1, FORCE], fx)
    pack_to = lax.broadcasted_iota(jnp.int32, (64, 256), 0)
    pack_from = lax.broadcasted_iota(jnp.int32, (64, 256), 1)
    pack = (pack_from == (pack_to // 2) * 8 + pack_to % 2).astype(F32).astype(BF16)
    packed = jnp.dot(pack, fx[...].reshape(256, LANES), preferred_element_type=F32)
    fz[zhi] = packed.astype(BF16)
    remote(fz.at[zhi], fz.at[zhi], 2, FORCE, z_peer)

    def forward(k, _):
        @pl.when(k + 2 < PIECES)
        def _():
            start_y(k + 2, v_ref.at[k + 2])

        start_x(k, xbuf.at[k, :, zhi])

        @pl.when(k > 1)
        def _():
            start_z(k - 1)

        return 0

    lax.fori_loop(1, PIECES, forward, 0)
    start_z(PIECES - 1)

    dx_copy.wait()

    def along_x(n, _):
        cols = pl.ds(pl.multiple_of(n * 256, 256), 256)
        total = jnp.zeros((192, 256), F32)
        for q in range(3):
            lhs = v_ref[3 * q : 3 * q + 3].reshape(192, WIDE)
            total += jnp.dot(lhs, dx[q * WIDE : (q + 1) * WIDE, cols], preferred_element_type=F32)
        ax[:, cols] = total * mx_ref[:, cols]
        return 0

    lax.fori_loop(0, 6, along_x, 0)

    wait_for(recv.at[2, FORCE], fz.at[1 - zhi])
    wait_for(recv.at[5, 1], rm_x)
    named = rm_x[...].reshape(256, LANES).astype(F32)
    lane = lax.broadcasted_iota(jnp.int32, (256, LANES), 1)
    coarse_row = ((lane % 64) // 2) * 4 + (lane // 64) * 2 + lane % 2
    choice = (named == coarse_row.astype(F32)).astype(F32).astype(BF16)
    picked = jnp.dot(choice, fz[...].reshape(LANES, LANES), preferred_element_type=F32)
    zbuf[FORCE] = picked.astype(BF16).reshape(NXD * NYD, 8, LANES)
    start_back_x(FORCE)

    cell = lax.broadcasted_iota(jnp.int32, (256, WIDE), 0)
    for q in range(3):
        cols = slice(q * WIDE, (q + 1) * WIDE)
        left = xw_ref[:, cols]
        right = (1.0 - left).astype(BF16).astype(F32)
        index = xi_ref[:, cols]
        table[:, cols] = (
            jnp.where(cell == index, left, 0.0) + jnp.where(cell == index + 1, right, 0.0)
        ).astype(BF16)

    start_back_y(FORCE)

    def turn(k):
        wait_for(recv.at[2, k], xbuf.at[k, :, 1 - zhi])
        slope = jnp.dot(
            dy_ref[:, zhi].reshape(256, 512), xbuf[k].reshape(512, LANES),
            preferred_element_type=F32,
        )
        zbuf[k] = (slope * metric).astype(BF16).reshape(NXD * NYD, 8, LANES)
        start_back_x(k)

    turn(0)
    wait_back_y(FORCE)
    remote(rybuf.at[FORCE, 0:2], rim, 5, 2, below)
    turn(1)
    start_back_y(0)

    wait_for(recv.at[5, 2], rim)
    topmost = slab == slabs - 1
    for c in range(3):
        cols = slice(c * LANES, (c + 1) * LANES)
        for h in range(2):
            levels = [rybuf[FORCE, 2 * m + h, :, cols].astype(F32) for m in range(4)]
            levels.append(jnp.where(topmost, levels[3], rim[h, :, cols].astype(F32)))
            for m in range(4):
                out = slice(h * LANES, (h + 1) * LANES)
                chosen[c * 8 + 2 * m, :, out] = levels[m].astype(BF16)
                chosen[c * 8 + 2 * m + 1, :, out] = (0.5 * (levels[m] + levels[m + 1])).astype(BF16)

    def upsample(n, _):
        cols = pl.ds(pl.multiple_of(n * 256, 256), 256)
        forcing[:, cols] = jnp.dot(
            chosen[...].reshape(192, 256), table[:, cols], preferred_element_type=F32
        )
        return 0

    lax.fori_loop(0, 6, upsample, 0)

    def finish(q):
        u = v_ref[3 * q].astype(F32).reshape(64, WIDE)
        v = v_ref[3 * q + 1].astype(F32).reshape(64, WIDE)
        for c in range(3):
            k = 3 * q + c
            wait_back_y(k)
            rows = slice(64 * c, 64 * c + 64)
            cols = slice(q * WIDE, (q + 1) * WIDE)
            along_y = rybuf[k].astype(F32).reshape(64, WIDE)
            own = v_ref[k].astype(F32).reshape(64, WIDE)
            t = forcing[rows, cols] - (u * ax[rows, cols] + v * along_y)
            tend_ref[k] = t.astype(BF16).reshape(8, 8, WIDE)
            upd_ref[k] = (own + rk_weight * t).astype(BF16).reshape(8, 8, WIDE)

    for k in range(2, PIECES):
        turn(k)
        start_back_y(k - 1)
        if k == 4:
            finish(0)
        if k == 7:
            finish(1)
    start_back_y(PIECES - 1)

    def sent(k, _):
        wait_for(send.at[0, k], ybuf.at[k, 0 : NYD - 1])
        wait_for(send.at[1, k], xbuf.at[0, 0 : 8 * (NXD - 1), 0])
        wait_for(send.at[3, k], xbuf.at[0, 0 : 8 * (NXD - 1), 0])
        return 0

    lax.fori_loop(0, PIECES + 1, sent, 0)

    def sent_z(k, _):
        wait_for(send.at[2, k], xbuf.at[k, :, zhi])
        return 0

    lax.fori_loop(0, PIECES, sent_z, 0)
    wait_for(send.at[2, FORCE], fz.at[zhi])
    wait_for(send.at[5, 0], rm_y.at[0 : NYD - 1])
    wait_for(send.at[5, 1], rm_x.at[0 : 8 * (NXD - 1)])
    wait_for(send.at[5, 2], rim)

    finish(2)

    def sent_y(k, _):
        wait_for(send.at[4, k], rybuf.at[k, 0 : NYD - 1])
        return 0

    lax.fori_loop(0, PIECES + 1, sent_y, 0)


def shards(
    velocity, deriv_x, deriv_y, metric_x, metric_y, coarse_force, row_map, x_index, x_weight
):
    rows, levels, components, width = velocity.shape
    pieces = velocity.reshape(rows, levels, components, 3, WIDE).transpose(3, 2, 1, 0, 4)
    pieces = pieces.reshape(PIECES, levels, rows, WIDE)
    coarse = jnp.pad(coarse_force, ((0, 6), (0, 0), (0, 1), (0, 64)))
    coarse = coarse.reshape(8, 4, 4, 2, LANES).transpose(1, 3, 0, 2, 4).reshape(8, 8, WIDE)
    named = jnp.broadcast_to(row_map.astype(F32).astype(BF16)[:, None], (8, LANES))
    vmem = pl.BlockSpec(memory_space=pltpu.VMEM)
    out = jax.ShapeDtypeStruct((PIECES, 8, 8, WIDE), BF16)
    tend, upd = pl.pallas_call(
        kernel,
        out_shape=(out, out),
        in_specs=[vmem] * 8 + [pl.BlockSpec(memory_space=pltpu.HBM)],
        out_specs=(vmem, vmem),
        scratch_shapes=[
            pltpu.VMEM((width, width), BF16),
            pltpu.VMEM((PIECES + 1, 8, 8, WIDE), BF16),
            pltpu.VMEM((PIECES, 32, 2, 8, LANES), BF16),
            pltpu.VMEM((32, 8, LANES), BF16),
            pltpu.VMEM((2, 64, LANES), BF16),
            pltpu.VMEM((PIECES + 1, 32, 8, LANES), BF16),
            pltpu.VMEM((PIECES + 1, 8, 8, WIDE), BF16),
            pltpu.VMEM((PIECES + 1, 8, 8, WIDE), BF16),
            pltpu.VMEM((2, 8, WIDE), BF16),
            pltpu.VMEM((8, 8, LANES), BF16),
            pltpu.VMEM((32, 8, LANES), BF16),
            pltpu.VMEM((192, width), F32),
            pltpu.VMEM((24, 8, 256), BF16),
            pltpu.VMEM((256, width), BF16),
            pltpu.VMEM((192, width), F32),
            pltpu.SemaphoreType.DMA((6, PIECES + 1)),
            pltpu.SemaphoreType.DMA((6, PIECES + 1)),
            pltpu.SemaphoreType.DMA,
        ],
        compiler_params=pltpu.CompilerParams(
            collective_id=0, has_side_effects=True, vmem_limit_bytes=48 << 20
        ),
    )(
        pieces,
        coarse,
        named,
        deriv_y.reshape(32, 2, 8, 512),
        metric_y.reshape(1, -1),
        metric_x.reshape(1, -1),
        x_index.reshape(1, -1),
        x_weight.astype(F32).reshape(1, -1),
        deriv_x,
    )

    def natural(a):
        a = a.reshape(3, components, levels, rows, WIDE).transpose(3, 2, 1, 0, 4)
        return a.reshape(velocity.shape)

    return natural(tend), natural(upd)


def solution(mesh):
    return jax.shard_map(
        shards,
        mesh=mesh,
        in_specs=(
            P("row", "slab", None, None), P(), P(), P(), P(),
            P("row", "slab", None, None), P("row"), P(), P(),
        ),
        out_specs=(P("row", "slab", None, None), P("row", "slab", None, None)),
        check_vma=False,
    )
```

time: 237 us -> 102 us (0.43); the launches traced: 233 us -> 101 us
  waiting for transfers between devices: 156 us -> 0 us
  Pallas kernels: 0 us -> 92 us
  starting transfers between devices: 44.5 us -> 0 us
  between operations: 14.3 us -> 0.66 us
  matrix products: 6.53 us -> 0 us
  local copies, waits for them, and re-layouts: 11.5 us -> 7.91 us
    all_gather x1 -> x0, waiting for transfers between devices: 136 us -> none  [shards(): portion = lax.all_gather(fine_source, 'row', axis=0, tiled=True)]
    pallas_call x0 -> x1, Pallas kernels: none -> 92 us  [shards(): pl.pallas_call(kernel, out_shape=(out, out), in_specs=[vmem] * 8 + [pl.Bl...]
    all_to_all x2 -> x0, starting transfers between devices: 41.6 us -> none  [the longest x1 23.8 us: shards(): lax.all_to_all(flattened, 'row', split_axis=1, concat_axis=0, tiled=True)]
    ppermute x1 -> x0, waiting for transfers between devices: 20 us -> none  [passed_along(): return lax.ppermute(block, axis, route)]
    dot_general x4 -> x0, matrix products: 6.53 us -> none  [the longest x1 4.07 us: shards(): jnp.dot(velocity.reshape(-1, fine_width), deriv_x, preferred_element_type...]
    convert_element_type x3 -> x0, local copies, waits for them, and re-layouts: 3.46 us -> none  [the longest x2 2.38 us: shards(): along_y.astype(jnp.float32)]
    ppermute x1 -> x0, starting transfers between devices: 2.86 us -> none  [passed_along(): return lax.ppermute(block, axis, route)]
    reshape x1 -> x6, local copies, waits for them, and re-layouts: 0.61 us -> 3.42 us  [the longest x1 1.26 us: shards(): velocity.reshape(rows, levels, components, 3, WIDE).transpose(3, 2, 1, 0, 4)]
  transfers between devices with their start and end apart: 4 -> 0, of which waited for: 2 -> 0; matrix products, arithmetic and copies ran while one was open for 3% -> 0% of each run, Pallas kernels for 0% -> 0%
where the time goes in v1:
time: 102 us; the launch traced here: 101 us
  Pallas kernels  92 us (90%)
  local copies, waits for them, and re-layouts  7.91 us (8%)
    pallas_call x1, Pallas kernels, shards(): pl.pallas_call(kernel, out_shape=(out, out), in_specs=[vmem] * 8 + [pl.Bl...  92 us

profile of v1, /device:TPU:1, one launch (start us, length us, event | category | flops | bytes accessed | tf_op | source)
XLA Modules:
  0.0 101.2 jit_solution(17092265348296659394)
XLA Ops:
  0.6 0.7 convert_convert_fusion
  1.3 0.1 broadcast_in_dim.2.rowmap_ref
  1.4 0.7 reshape.52.mx_ref
  2.1 0.7 reshape.53.xi_ref
  2.8 0.7 reshape.61.xw_ref
  3.5 0.7 pad.4
  4.3 1.3 %copy.11 = bf16[8,8,3,3,512]{4,0,1,2,3:T(8,128)(2,1)S(1)} copy(bf16[8,8,3,3,512]{4,1,3,2,0:T(8,128)(2,1)} %bitcast.25) | data formatting | bytes 1179648 | tf_op jit(solution)/shard_map/reshape | solution.py:268
  5.5 0.0 copy-start
  5.5 1.0 %copy-done = bf16[512,512]{1,0:T(8,128)(2,1)S(1)} copy-done((bf16[512,512]{1,0:T(8,128)(2,1)S(1)}, bf16[512,512]{1,0:T(8,128)(2,1)}, u32[]{:S(2)}) %copy-start) | copy-done | bytes 524312
  6.6 0.0 copy-start.1
  6.6 0.7 copy-done.1
  7.3 92.0 %shard_map.104 = (bf16[9,8,8,512]{3,2,1,0:T(8,128)(2,1)S(1)}, bf16[9,8,8,512]{3,2,1,0:T(8,128)(2,1)S(1)}) custom-call(bf16[9,8,8,512]{3,2,1,0:T(8,128)(2,1)S(1)} %bitcast.19, bf16[8,8,512]{2,1,0:T(8,128)(2,1)S(1)} %bitcast.23, bf16[8,128]{1,0:T(8,128)(2,1)S(1)} %broadcast_in_dim.2.rowmap_ref, bf16[32,2,8,512]{3,2,1,0:T(8,128)(2,1)S(1)} %bitcast.22, ...), custom_call_target="tpu_custom_call" | custom-call | tf_op jit(solution)/shard_map/pallas_call | solution.py:275
  99.2 1.0 copy.13
  100.2 1.0 copy.14
  (2 shorter events, 0.1 us)
Async XLA Ops:
  5.5 1.0 %copy-start = (bf16[512,512]{1,0:T(8,128)(2,1)S(1)}, bf16[512,512]{1,0:T(8,128)(2,1)}, u32[]{:S(2)}) copy-start(bf16[512,512]{1,0:T(8,128)(2,1)} %param.11) | copy-start | bytes 1572868
  6.6 0.7 copy-start.1

commit v2 on v0

v2 whole, which is shorter than its diff:
```python
import jax
import jax.numpy as jnp
from jax import lax
from jax.experimental import pallas as pl
from jax.experimental.pallas import tpu as pltpu
from jax.sharding import PartitionSpec as P

rk_weight = 0.5
MESH = pl.DeviceIdType.MESH
F32 = jnp.float32
BF16 = jnp.bfloat16

NXD, NYD = 4, 8
LANES = 128
WIDE = NXD * LANES
PIECES = 9
FORCE = PIECES
EXTRA = FORCE + 1
MID, REST = (0, 2), (2, 5)
FIRST = (5, 7)
LAST = (7, 9)


def kernel(
    v_hbm, coarse_ref, const_ref, dy_hbm, dx_hbm,
    tend_ref, upd_ref,
    v_ref, dy_ref, dx, xbuf, fx, fz, zbuf, fback, rybuf, zfirst, zlast, rim,
    ax, chosen, table, forcing,
    send, recv, load_sem,
):
    slab = lax.axis_index("slab")
    row = lax.axis_index("row")
    slabs = lax.axis_size("slab")
    zhi = row % 2
    y = (row // 2) % NYD
    x = row // (2 * NYD)
    place = x * NYD + y

    plane = []
    for i in range(NXD):
        for j in range(NYD):
            if i or j:
                px, py = lax.rem(x + i, NXD), lax.rem(y + j, NYD)
                plane.append((px, py, (slab, (px * NYD + py) * 2 + zhi)))
    z_peer = (slab, place * 2 + 1 - zhi)
    below = (lax.rem(slab + slabs - 1, slabs), row)
    above = (lax.rem(slab + 1, slabs), row)

    barrier = pltpu.get_barrier_semaphore()
    greeted = [device for _, _, device in plane] + [z_peer, below, above]
    for device in greeted:
        pl.semaphore_signal(barrier, inc=1, device_id=device, device_id_type=MESH)

    loads = [
        pltpu.make_async_copy(v_hbm, v_ref, load_sem.at[0]),
        pltpu.make_async_copy(dy_hbm, dy_ref, load_sem.at[1]),
        pltpu.make_async_copy(dx_hbm, dx, load_sem.at[2]),
    ]
    for load in loads:
        load.start()
    pl.semaphore_wait(barrier, len(greeted))

    left = []

    def remote(src, dst, stage, slot, device):
        pltpu.make_async_remote_copy(
            src_ref=src, dst_ref=dst, send_sem=send.at[stage, slot], recv_sem=recv.at[stage, slot],
            device_id=device, device_id_type=MESH,
        ).start()

    def local(src, dst, stage, slot):
        pltpu.make_async_copy(src, dst, recv.at[stage, slot]).start()

    def wait_for(sem, part):
        pltpu.make_async_copy(part, part, sem).wait()

    def quarter(i):
        return pl.ds(pl.multiple_of(i * LANES, LANES), LANES)

    def span(group):
        return slice(*group)

    def out(slot, src, dst, count):
        for i, j, device in plane:
            remote(src.at[:, j, :, quarter(i)], dst.at[:, place], 0, slot, device)
        local(src.at[:, y, :, quarter(x)], dst.at[:, place], 0, slot)
        left.append((0, slot, zbuf.at[0:count, 0:31]))

    def wait_out(slot, dst):
        wait_for(recv.at[0, slot], dst)

    def cross(slot, src, dst):
        remote(src, dst, 1, slot, z_peer)
        left.append((1, slot, dst))

    def wait_cross(slot, dst):
        wait_for(recv.at[1, slot], dst)

    def back(slot, src, dst, count):
        for i, j, device in plane:
            remote(src.at[:, i * NYD + j], dst.at[:, y, :, quarter(x)], 2, slot, device)
        local(src.at[:, place], dst.at[:, y, :, quarter(x)], 2, slot)
        left.append((2, slot, zbuf.at[0:count, 0:31]))

    def wait_back(slot, dst):
        wait_for(recv.at[2, slot], dst)

    def half(group, side):
        return xbuf.at[span(group), :, side]

    cross(2, v_hbm.at[span(FIRST)], zfirst)
    out(0, v_hbm.at[span(MID)], half(MID, zhi), 2)
    out(4, coarse_ref, fx, 1)
    out(1, v_hbm.at[span(REST)], half(REST, zhi), 3)
    out(3, v_hbm.at[span(LAST)], half(LAST, zhi), 2)

    block = lax.broadcasted_iota(jnp.int32, (32, 8, 512), 0)
    inner = lax.broadcasted_iota(jnp.int32, (32, 8, 512), 1)
    lane = lax.broadcasted_iota(jnp.int32, (32, 8, 512), 2)
    y_metric = const_ref[3:4, 0:512].reshape(1, 1, 512)
    metric = [
        jnp.sum(
            jnp.where(lane == block * 16 + inner + side * 8, y_metric, 0.0), axis=2, keepdims=True
        )
        for side in (zhi, 1 - zhi)
    ]
    pack_to = lax.broadcasted_iota(jnp.int32, (64, 256), 0)
    pack_from = lax.broadcasted_iota(jnp.int32, (64, 256), 1)
    pack = (pack_from == (pack_to >> 1) * 8 + (pack_to & 1)).astype(F32).astype(BF16)
    for k in range(*LAST):
        xbuf[k, :, 1 - zhi] = jnp.zeros((32, 8, LANES), BF16)

    wait_out(0, half(MID, zhi))
    cross(0, half(MID, zhi), half(MID, zhi))

    wait_out(4, fx)
    packed = jnp.dot(pack, fx[0].reshape(256, LANES), preferred_element_type=F32)
    fz[zhi] = packed.astype(BF16)
    cross(4, fz.at[zhi], fz.at[zhi])

    wait_out(1, half(REST, zhi))
    cross(1, half(REST, zhi), half(REST, zhi))

    wait_cross(2, zfirst)
    out(5, zfirst, half(FIRST, 1 - zhi), 2)
    out(2, v_hbm.at[span(FIRST)], half(FIRST, zhi), 2)

    for load in loads:
        load.wait()

    def along_x(n):
        cols = slice(n * 256, (n + 1) * 256)
        total = jnp.zeros((192, 256), F32)
        for q in range(3):
            lhs = v_ref[3 * q : 3 * q + 3].reshape(192, WIDE)
            total += jnp.dot(lhs, dx[q * WIDE : (q + 1) * WIDE, cols], preferred_element_type=F32)
        ax[:, cols] = total * const_ref[0:1, cols]

    def slope(k, half):
        out = jnp.dot(
            dy_ref[:, zhi if half == 0 else 1 - zhi].reshape(256, 512),
            xbuf[k].reshape(512, LANES),
            preferred_element_type=F32,
        )
        return (out.reshape(32, 8, LANES) * metric[half]).astype(BF16)

    def fill_table(q):
        cell = lax.broadcasted_iota(jnp.int32, (256, WIDE), 0).astype(F32)
        cols = slice(q * WIDE, (q + 1) * WIDE)
        weight = const_ref[2:3, cols]
        rest = (1.0 - weight).astype(BF16).astype(F32)
        index = const_ref[1:2, cols]
        table[:, cols] = (
            jnp.where(cell == index, weight, 0.0) + jnp.where(cell == index + 1.0, rest, 0.0)
        ).astype(BF16)

    def turn(group):
        for k in range(*group):
            zbuf[k] = slope(k, 0)

    wait_out(3, half(LAST, zhi))
    for b, k in enumerate(range(*LAST)):
        zbuf[EXTRA + b] = slope(k, 1)
    back(6, zbuf.at[EXTRA : EXTRA + 2], rybuf.at[EXTRA - 1 : EXTRA + 1], 2)
    turn(LAST)
    back(3, zbuf.at[span(LAST)], rybuf.at[span(LAST)], 2)

    wait_cross(4, fz.at[1 - zhi])
    lane = lax.broadcasted_iota(jnp.int32, (32, 8, LANES), 2)
    inner = lax.broadcasted_iota(jnp.int32, (32, 8, LANES), 1)
    named = fx[0].astype(F32)[:, 2:3, :]
    named = jnp.sum(jnp.where(lane == inner, named, 0.0), axis=2, keepdims=True)
    coarse_row = ((lane & 63) >> 1) * 4 + (lane >> 6) * 2 + (lane & 1)
    choice = jnp.where(named == coarse_row.astype(F32), 1.0, 0.0).reshape(256, LANES).astype(BF16)
    picked = jnp.dot(choice, fz[...].reshape(LANES, LANES), preferred_element_type=F32)
    zbuf[FORCE] = picked.reshape(32, 8, LANES).astype(BF16)
    back(4, zbuf.at[FORCE:EXTRA], fback, 1)

    wait_back(6, rybuf.at[EXTRA - 1 : EXTRA + 1])
    cross(3, rybuf.at[EXTRA - 1 : EXTRA + 1], zlast)

    wait_out(5, half(FIRST, 1 - zhi))
    wait_out(2, half(FIRST, zhi))
    turn(FIRST)
    back(2, zbuf.at[span(FIRST)], rybuf.at[span(FIRST)], 2)

    wait_back(4, fback)
    remote(fback.at[0, 0:2], rim, 3, 0, below)
    left.append((3, 0, rim))

    wait_cross(0, half(MID, 1 - zhi))
    turn(MID)
    back(0, zbuf.at[span(MID)], rybuf.at[span(MID)], 2)

    def refine():
        wait_for(recv.at[3, 0], rim)
        topmost = slab == slabs - 1
        for c in range(3):
            cols = slice(c * LANES, (c + 1) * LANES)
            for h in range(2):
                levels = [fback[0, 2 * m + h, :, cols].astype(F32) for m in range(4)]
                levels.append(jnp.where(topmost, levels[3], rim[h, :, cols].astype(F32)))
                for m in range(4):
                    to = slice(h * LANES, (h + 1) * LANES)
                    chosen[c * 8 + 2 * m, :, to] = levels[m].astype(BF16)
                    half_way = 0.5 * (levels[m] + levels[m + 1])
                    chosen[c * 8 + 2 * m + 1, :, to] = half_way.astype(BF16)

    def upsample(n):
        cols = slice(n * 256, (n + 1) * 256)
        forcing[:, cols] = jnp.dot(
            chosen[...].reshape(192, 256), table[:, cols], preferred_element_type=F32
        )

    def finish(k):
        q, c = k // 3, k % 3
        rows = slice(64 * c, 64 * c + 64)
        cols = slice(q * WIDE, (q + 1) * WIDE)
        u = v_ref[3 * q].astype(F32).reshape(64, WIDE)
        v = v_ref[3 * q + 1].astype(F32).reshape(64, WIDE)
        along_y = rybuf[k].astype(F32).reshape(64, WIDE)
        if k >= LAST[0]:
            along_y += zlast[k - LAST[0]].astype(F32).reshape(64, WIDE)
            along_y = along_y.astype(BF16).astype(F32)
        here = v_ref[k].astype(F32).reshape(64, WIDE)
        t = forcing[rows, cols] - (u * ax[rows, cols] + v * along_y)
        tend_ref[k] = t.astype(BF16).reshape(8, 8, WIDE)
        upd_ref[k] = (here + rk_weight * t).astype(BF16).reshape(8, 8, WIDE)

    for q in range(3):
        fill_table(q)
    refine()
    for n in range(6):
        along_x(n)
        upsample(n)

    wait_cross(1, half(REST, 1 - zhi))
    turn(REST)
    back(1, zbuf.at[span(REST)], rybuf.at[span(REST)], 3)

    wait_back(0, rybuf.at[span(MID)])
    wait_back(2, rybuf.at[span(FIRST)])
    wait_back(3, rybuf.at[span(LAST)])
    for k in (*range(*MID), *range(*FIRST)):
        finish(k)
    for stage, slot, part in left:
        if (stage, slot) not in ((1, 3), (2, 1)):
            wait_for(send.at[stage, slot], part)
    wait_back(1, rybuf.at[span(REST)])
    for k in range(*REST):
        finish(k)
    wait_cross(3, zlast)
    for k in range(*LAST):
        finish(k)
    for stage, slot, part in left:
        if (stage, slot) in ((1, 3), (2, 1)):
            wait_for(send.at[stage, slot], part)


def shards(
    velocity, deriv_x, deriv_y, metric_x, metric_y, coarse_force, row_map, x_index, x_weight
):
    rows, levels, components, width = velocity.shape
    pieces = velocity.reshape(rows, levels, components, 3, WIDE).transpose(3, 2, 1, 0, 4)
    pieces = pieces.reshape(PIECES, levels, rows, WIDE)
    coarse = jnp.pad(coarse_force, ((0, 6), (0, 0), (0, 1), (0, 64)))
    coarse = coarse.reshape(8, 4, 4, 2, LANES).transpose(1, 3, 0, 2, 4).reshape(8, 8, WIDE)
    named = jnp.tile(jnp.pad(row_map.astype(F32), (0, LANES - rows)), 4)[None, None, :]
    third_row = lax.broadcasted_iota(jnp.int32, (8, 8, WIDE), 1) == 2
    coarse = jnp.where(third_row, named, coarse.astype(F32)).astype(BF16)[None]
    width_row = jnp.stack(
        [metric_x, x_index.astype(F32), x_weight.astype(F32), jnp.pad(metric_y, (0, width - 512))]
    )
    vmem = pl.BlockSpec(memory_space=pltpu.VMEM)
    hbm = pl.BlockSpec(memory_space=pltpu.HBM)
    out = jax.ShapeDtypeStruct((PIECES, 8, 8, WIDE), BF16)
    tend, upd = pl.pallas_call(
        kernel,
        out_shape=(out, out),
        in_specs=[hbm, vmem, vmem, hbm, hbm],
        out_specs=(vmem, vmem),
        scratch_shapes=[
            pltpu.VMEM((PIECES, 8, 8, WIDE), BF16),
            pltpu.VMEM((32, 2, 8, 512), BF16),
            pltpu.VMEM((width, width), BF16),
            pltpu.VMEM((PIECES, 32, 2, 8, LANES), BF16),
            pltpu.VMEM((1, 32, 8, LANES), BF16),
            pltpu.VMEM((2, 64, LANES), BF16),
            pltpu.VMEM((EXTRA + 2, 32, 8, LANES), BF16),
            pltpu.VMEM((1, 8, 8, WIDE), BF16),
            pltpu.VMEM((PIECES + 2, 8, 8, WIDE), BF16),
            pltpu.VMEM((2, 8, 8, WIDE), BF16),
            pltpu.VMEM((2, 8, 8, WIDE), BF16),
            pltpu.VMEM((2, 8, WIDE), BF16),
            pltpu.VMEM((192, width), F32),
            pltpu.VMEM((24, 8, 256), BF16),
            pltpu.VMEM((256, width), BF16),
            pltpu.VMEM((192, width), F32),
            pltpu.SemaphoreType.DMA((4, 8)),
            pltpu.SemaphoreType.DMA((4, 8)),
            pltpu.SemaphoreType.DMA((3,)),
        ],
        compiler_params=pltpu.CompilerParams(
            collective_id=0, has_side_effects=True, vmem_limit_bytes=48 << 20
        ),
    )(pieces, coarse, width_row, deriv_y.reshape(32, 2, 8, 512), deriv_x)

    def natural(a):
        a = a.reshape(3, components, levels, rows, WIDE).transpose(3, 2, 1, 0, 4)
        return a.reshape(velocity.shape)

    return natural(tend), natural(upd)


def solution(mesh):
    return jax.shard_map(
        shards,
        mesh=mesh,
        in_specs=(
            P("row", "slab", None, None), P(), P(), P(), P(),
            P("row", "slab", None, None), P("row"), P(), P(),
        ),
        out_specs=(P("row", "slab", None, None), P("row", "slab", None, None)),
        check_vma=False,
    )
```

time: 237 us -> 80.7 us (0.34); the launches traced: 233 us -> 80.3 us
  waiting for transfers between devices: 156 us -> 0 us
  Pallas kernels: 0 us -> 71 us
  starting transfers between devices: 44.5 us -> 0 us
  between operations: 14.3 us -> 0.67 us
  matrix products: 6.53 us -> 0 us
  local copies, waits for them, and re-layouts: 11.5 us -> 7.18 us
    all_gather x1 -> x0, waiting for transfers between devices: 136 us -> none  [shards(): portion = lax.all_gather(fine_source, 'row', axis=0, tiled=True)]
    pallas_call x0 -> x1, Pallas kernels: none -> 71 us  [shards(): pl.pallas_call(kernel, out_shape=(out, out), in_specs=[hbm, vmem, vmem, h...]
    all_to_all x2 -> x0, starting transfers between devices: 41.6 us -> none  [the longest x1 23.8 us: shards(): lax.all_to_all(flattened, 'row', split_axis=1, concat_axis=0, tiled=True)]
    ppermute x1 -> x0, waiting for transfers between devices: 20 us -> none  [passed_along(): return lax.ppermute(block, axis, route)]
    dot_general x4 -> x0, matrix products: 6.53 us -> none  [the longest x1 4.07 us: shards(): jnp.dot(velocity.reshape(-1, fine_width), deriv_x, preferred_element_type...]
    ppermute x1 -> x0, starting transfers between devices: 2.86 us -> none  [passed_along(): return lax.ppermute(block, axis, route)]
    convert_element_type x3, local copies, waits for them, and re-layouts: 3.46 us -> 0.79 us  [shards(): coarse = jnp.where(third_row, named, coarse.astype(F32)).astype(BF16)[None]]
  transfers between devices with their start and end apart: 4 -> 0, of which waited for: 2 -> 0; matrix products, arithmetic and copies ran while one was open for 3% -> 0% of each run, Pallas kernels for 0% -> 0%
where the time goes in v2:
time: 80.7 us; the launch traced here: 80.3 us
  Pallas kernels  71 us (88%)
  local copies, waits for them, and re-layouts  7.18 us (9%)
  other arithmetic  1.47 us (2%)
    pallas_call x1, Pallas kernels, shards(): pl.pallas_call(kernel, out_shape=(out, out), in_specs=[hbm, vmem, vmem, h...  71 us
    transpose x2, local copies, waits for them, and re-layouts, natural(): a = a.reshape(3, components, levels, rows, WIDE).transpose(3, 2, 1, 0, 4)  1.98 us

profile of v2, /device:TPU:1, one launch (start us, length us, event | category | flops | bytes accessed | tf_op | source)
XLA Modules:
  0.0 80.3 jit_solution(16614064956168600979)
XLA Ops:
  0.6 0.7 convert_element_type.42
  1.3 0.7 stack.18
  2.0 0.7 reshape.57
  2.7 0.7 pad.14
  3.4 0.7 convert_element_type.48
  4.1 0.7 pad_convert_fusion
  4.9 0.1 select_convert_fusion.coarse_ref
  5.0 1.3 %copy.11 = bf16[8,8,3,3,512]{4,0,1,2,3:T(8,128)(2,1)S(1)} copy(bf16[8,8,3,3,512]{4,1,3,2,0:T(8,128)(2,1)} %bitcast.24) | data formatting | bytes 1179648 | tf_op jit(solution)/shard_map/reshape | solution.py:284
  6.3 0.0 copy-start
  6.3 1.0 %copy-done = bf16[512,512]{1,0:T(8,128)(2,1)S(1)} copy-done((bf16[512,512]{1,0:T(8,128)(2,1)S(1)}, bf16[512,512]{1,0:T(8,128)(2,1)}, u32[]{:S(2)}) %copy-start) | copy-done | bytes 524312
  7.3 71.0 %shard_map.104 = (bf16[9,8,8,512]{3,2,1,0:T(8,128)(2,1)S(1)}, bf16[9,8,8,512]{3,2,1,0:T(8,128)(2,1)S(1)}) custom-call(bf16[9,8,8,512]{3,2,1,0:T(8,128)(2,1)S(1)} %bitcast.20, bf16[1,8,8,512]{3,2,1,0:T(8,128)(2,1)S(1)} %select_convert_fusion.coarse_ref, f32[4,1536]{1,0:T(4,128)S(1)} %pad_maximum_fusion.const_ref, bf16[32,2,8,512]{3,2,1,0:T(8,128)(2,1)S(1)} %bitcast.23, ...), custom_call_target="tpu_custom_call" | custom-call | tf_op jit(solution)/shard_map/pallas_call | solution.py:297
  78.3 1.0 %copy.13 = bf16[8,8,3,3,512]{4,1,3,2,0:T(8,128)(2,1)} copy(bf16[8,8,3,3,512]{4,0,1,2,3:T(8,128)(2,1)S(1)} %bitcast.22) | data formatting | bytes 1179648 | tf_op jit(solution)/shard_map/transpose | solution.py:329
  79.3 1.0 %copy.14 = bf16[8,8,3,3,512]{4,1,3,2,0:T(8,128)(2,1)} copy(bf16[8,8,3,3,512]{4,0,1,2,3:T(8,128)(2,1)S(1)} %bitcast.21) | data formatting | bytes 1179648 | tf_op jit(solution)/shard_map/transpose | solution.py:329
  (8 shorter events, 0.1 us)
Async XLA Ops:
  6.3 1.0 %copy-start = (bf16[512,512]{1,0:T(8,128)(2,1)S(1)}, bf16[512,512]{1,0:T(8,128)(2,1)}, u32[]{:S(2)}) copy-start(bf16[512,512]{1,0:T(8,128)(2,1)} %param.11) | copy-start | bytes 1572868
